TPU v7x, 256 devices: a whole 4x4x8 slice. The times are simulated.
256 devices in a mesh: layer: 64 (over y, x_lo, z), feat: 4 (over x_hi, core).
Axes of the slice: x: 4 (x_hi: 2, x_lo: 2; x = x_hi * 2 + x_lo), y: 4, z: 8, core: 2. Of those that a mesh axis runs over, the one named last changes fastest.
Arguments:
- sources: bfloat16 [256, 8192], P(('layer', 'feat')), may hold values from -6 to 6
- targets: bfloat16 [256, 16384], P(('layer', 'feat')), may hold values from -16 to 16
- enc_weight: bfloat16 [8192, 32768], P(None, ('feat', 'layer')), may hold values from -0.0625 to 0.0625
- enc_bias: float32 [32768], P(('feat', 'layer')), may hold values from -3 to 3
- dec_weight: bfloat16 [32768, 16384], P('feat', 'layer'), may hold values from -0.03125 to 0.03125
- dec_bias: float32 [16384], P('layer'), may hold values from -3 to 3
Outputs:
- enc_grad: bfloat16 [8192, 32768], P(None, ('feat', 'layer'))
- dec_grad: bfloat16 [32768, 16384], P('feat', 'layer')
- mse: float32 [], replicated
All inputs are finite; a program needn't handle non-finite values.
Results may differ from a plain program's by a relative error of at most 0.011.
Values may be sent and summed in bfloat16 or wider, within the bound.
No kernel may reach another device: no remote copies, remote signals or barrier semaphores. Data moves between devices by JAX's collectives and lax.ppermute only.
A program may use at most 128 MiB of HBM per device.

v0:
```python
import math

import jax
import jax.numpy as jnp
from jax import lax
from jax.sharding import PartitionSpec as P


def per_device(sources, targets, enc_weight, enc_bias, dec_weight, dec_bias):
    inputs = lax.all_gather(sources, ("layer", "feat"), axis=0, tiled=True)
    tokens = inputs.shape[0]
    preact = jnp.dot(inputs, enc_weight, preferred_element_type=jnp.float32) + enc_bias
    feats = jax.nn.gelu(preact).astype(jnp.bfloat16)
    n_layer = lax.axis_size("layer")
    width = dec_weight.shape[1]
    spread = lax.all_gather(targets, "feat", axis=0, tiled=True)
    blocks = spread.reshape(spread.shape[0], n_layer, width)
    owned = lax.all_to_all(blocks, "layer", split_axis=1, concat_axis=0, tiled=True)
    wanted = owned.reshape(tokens, width)
    all_feats = lax.all_gather(feats, "layer", axis=1, tiled=True)
    partial_value = jnp.dot(all_feats, dec_weight, preferred_element_type=jnp.float32)
    factor = 1.0 / math.sqrt(tokens)
    outputs = lax.psum(partial_value.astype(jnp.bfloat16), "feat").astype(jnp.float32) + dec_bias
    misfit = outputs - wanted.astype(jnp.float32)
    errors = (misfit * factor).astype(jnp.bfloat16)
    total_sq = lax.psum(jnp.sum(misfit * misfit), "layer")
    mse = total_sq / (tokens * n_layer * width)
    dec_grad = lax.dot_general(
        all_feats, errors, (((0,), (0,)), ((), ())), preferred_element_type=jnp.float32
    ).astype(jnp.bfloat16)
    grad_rows = lax.psum_scatter(
        lax.dot_general(
            dec_weight, errors, (((1,), (1,)), ((), ())), preferred_element_type=jnp.float32
        ),
        "layer",
        scatter_dimension=0,
        tiled=True,
    )
    feat_grad = grad_rows.T
    _, pullback = jax.vjp(jax.nn.gelu, preact)
    pre_grad = pullback(feat_grad)[0].astype(jnp.bfloat16)
    enc_grad = lax.dot_general(
        inputs, pre_grad, (((0,), (0,)), ((), ())), preferred_element_type=jnp.float32
    ).astype(jnp.bfloat16)
    return (enc_grad, dec_grad, mse)


def solution(mesh):
    return jax.shard_map(
        per_device,
        mesh=mesh,
        in_specs=(
            P(("layer", "feat"), None),
            P(("layer", "feat"), None),
            P(None, ("feat", "layer")),
            P(("feat", "layer")),
            P("feat", "layer"),
            P("layer"),
        ),
        out_specs=(P(None, ("feat", "layer")), P("feat", "layer"), P()),
        check_vma=False,
    )
```

profile of v0, /device:TPU:4, one launch (start us, length us, event | category | flops | bytes accessed | tf_op | source)
XLA Modules:
  0.0 1093.3 jit_solution(547445359311050839)
XLA Ops:
  7.2 0.0 copy-start
  7.2 0.0 copy-start.1
  7.2 0.0 all-gather.7.cloned.1.call-start
  7.2 0.7 all-gather.7.cloned.1.call-update
  7.9 0.0 all-gather.5.cloned.1.call-start
  8.0 423.7 %all-gather.7.cloned.1.call-done = bf16[256,1,8192]{2,1,0:T(2,128)(2,1)} async-done(((bf16[1,1,8192]{2,1,0:T(2,128)(2,1)}), bf16[256,1,8192]{2,1,0:T(2,128)(2,1)}) %all-gather.7.cloned.1.call-update) | async-done | bytes 4194320 | tf_op jit(solution)/shard_map/all_gather | solution.py:10
  431.6 0.0 copy-done
  431.6 8.9 multiply_convert_fusion.1
  440.6 0.0 all-gather.5.cloned.1.call-update
  440.6 0.0 copy-done.1
  440.6 7.3 all-gather.1
  447.9 1.5 reduce
  449.3 7.6 all-to-all-start
  457.0 0.0 copy-start.2
  457.0 0.0 all-reduce.2.cloned.1.call-start
  457.0 224.1 %all-gather.5.cloned.1.call-done = bf16[256,8192]{1,0:T(8,128)(2,1)} async-done(((bf16[256,128]{1,0:T(8,128)(2,1)}), bf16[256,8192]{1,0:T(8,128)(2,1)}) %all-gather.5.cloned.1.call-update) | async-done | bytes 4194320 | tf_op jit(solution)/shard_map/all_gather | solution.py:20
  681.1 5.4 convolution_convert_fusion.2
  686.5 0.0 all-reduce.2.cloned.1.call-update
  686.5 0.0 reduce-scatter.2.cloned.1.call-start
  686.6 0.0 all-to-all-done
  686.6 0.1 reshape.18
  686.7 40.1 %all-reduce.2.cloned.1.call-done = bf16[256,256]{1,0:T(8,128)(2,1)} async-done(((bf16[256,256]{1,0:T(8,128)(2,1)}), bf16[256,256]{1,0:T(8,128)(2,1)}) %all-reduce.2.cloned.1.call-update) | async-done | bytes 131088 | tf_op jit(solution)/shard_map/psum | solution.py:23
  726.8 0.0 copy-done.2
  726.8 1.6 multiply_reduce_fusion
  728.4 6.7 convolution_bitcast_fusion
  735.1 0.0 reduce-scatter.2.cloned.1.call-update
  735.1 160.3 %psum.15 = f32[]{:T(128)} all-reduce(f32[]{:T(128)} %get-tuple-element.12), channel_id=1, replica_groups=mesh['layer'=64,'feat'=4] {'layer'}, use_global_device_ids=true, to_apply=%region_3.0 | all-reduce | flops 1 | bytes 8 | tf_op jit(solution)/shard_map/psum | solution.py:26
  896.1 5.5 convolution_convert_fusion
  901.7 170.2 %reduce-scatter.2.cloned.1.call-done = f32[128,256]{0,1:T(8,128)} async-done(((f32[8192,256]{0,1:T(8,128)}), f32[128,256]{0,1:T(8,128)}) %reduce-scatter.2.cloned.1.call-update) | async-done | bytes 131088 | tf_op jit(solution)/shard_map/reduce_scatter | solution.py:31
  1071.8 9.8 fusion
  1081.6 4.1 copy.13
  (1 shorter events, 0.0 us)
Async XLA Ops:
  7.2 424.5 %copy-start = (bf16[8192,128]{1,0:T(8,128)(2,1)S(1)}, bf16[8192,128]{1,0:T(8,128)(2,1)}, u32[]{:S(2)}) copy-start(bf16[8192,128]{1,0:T(8,128)(2,1)} %param.8) | copy-start | bytes 6291460
  7.2 433.4 %copy-start.1 = (bf16[1,16384]{1,0:T(2,128)(2,1)S(1)}, bf16[1,16384]{1,0:T(2,128)(2,1)}, u32[]{:S(2)}) copy-start(bf16[1,16384]{1,0:T(2,128)(2,1)} %param.7) | copy-start | bytes 98308
  7.2 424.4 %all-gather.7.cloned.1.call-start = ((), (), s32[]{:S(2)}) async-start(), calls=%async_computation.5 | async-start | bytes 8421376 | tf_op jit(solution)/shard_map/all_gather | solution.py:10
  7.9 673.2 %all-gather.5.cloned.1.call-start = ((), (), s32[]{:S(2)}) async-start(), calls=%async_computation.2 | async-start | bytes 4259840 | tf_op jit(solution)/shard_map/all_gather | solution.py:20
  449.3 237.3 %all-to-all-start = ((bf16[4,64,256]{2,0,1:T(4,128)(2,1)}), bf16[4,64,256]{2,0,1:T(4,128)(2,1)S(1)}, u32[]{:S(2)}, u32[]{:S(2)}) async-start(bf16[4,64,256]{2,0,1:T(4,128)(2,1)} %bitcast.9), calls=%async_computation | async-start | bytes 262144 | tf_op jit(solution)/shard_map/all_to_all | solution.py:18
  457.0 269.9 %copy-start.2 = (f32[256]{0:T(256)S(1)}, f32[256]{0:T(256)}, u32[]{:S(2)}) copy-start(f32[256]{0:T(256)} %param.11) | copy-start | bytes 3076
  457.0 269.8 %all-reduce.2.cloned.1.call-start = ((), (), s32[]{:S(2)}) async-start(), calls=%async_computation.3 | async-start | bytes 262144 | tf_op jit(solution)/shard_map/psum | solution.py:23
  686.5 385.3 %reduce-scatter.2.cloned.1.call-start = ((), (), s32[]{:S(2)}) async-start(), calls=%async_computation.4 | async-start | bytes 8519680 | tf_op jit(solution)/shard_map/reduce_scatter | solution.py:31
Sparse Core Ops, SparseCore 0:
  9.9 421.7 all-gather.6
  440.7 240.4 all-gather.4
  686.7 40.1 all-reduce.1
  735.3 336.4 reduce-scatter.1
where the time goes:
time: 1090 us
  waiting for transfers between devices  859 us (79%)
  blocking collectives  168 us (15%)
  matrix products  36.3 us (3%)
  between operations  15.6 us (1%)
    all_gather x1, waiting for transfers between devices, per_device(): inputs = lax.all_gather(sources, ('layer', 'feat'), axis=0, tiled=True)  424 us
    all_gather x1, waiting for transfers between devices, per_device(): all_feats = lax.all_gather(feats, 'layer', axis=1, tiled=True)  224 us
    reduce_scatter x1, waiting for transfers between devices, per_device(): lax.psum_scatter(lax.dot_general(dec_weight, errors, (((1,), (1,)), ((),...  170 us
    psum x1, blocking collectives, per_device(): total_sq = lax.psum(jnp.sum(misfit * misfit), 'layer')  160 us
    psum x1, waiting for transfers between devices, per_device(): lax.psum(partial_value.astype(jnp.bfloat16), 'feat').astype(jnp.float32)  40.1 us
  transfers between devices with their start and end apart: 5, of which 4 were waited for; matrix products, arithmetic and copies ran while one was open for 1% of the time, Pallas kernels for 0%

commit v1 on v0

v1 whole, which is shorter than its diff:
```python
import math

import jax
import jax.numpy as jnp
from jax import lax
from jax.sharding import Mesh, PartitionSpec as P

LAYER = ("y", "x_lo", "z")
FEAT = ("x_hi", "core")


def spread_to(block, axes):
    n = lax.axis_size(axes)
    return lax.all_to_all(
        jnp.broadcast_to(block[None], (n, *block.shape)), axes, split_axis=0, concat_axis=0, tiled=True
    )


def per_device(sources, targets, enc_weight, enc_bias, dec_weight, dec_bias):
    n_y, n_xl, n_z = (lax.axis_size(a) for a in LAYER)
    n_xh, n_c = (lax.axis_size(a) for a in FEAT)
    n_layer = n_y * n_xl * n_z
    rows, width = dec_weight.shape
    feats_own = enc_weight.shape[1]
    depth = sources.shape[1]
    tokens = n_layer * n_xh * n_c
    factor = 1.0 / math.sqrt(tokens)

    owned = lax.all_to_all(targets.reshape(n_layer, 1, width), LAYER, split_axis=0, concat_axis=0, tiled=True)
    wanted = lax.all_gather(owned.reshape(n_layer, width), FEAT, axis=0, tiled=True)
    wanted = wanted.reshape(n_xh, n_c, n_y * n_xl, n_z, width).transpose(1, 2, 0, 3, 4).reshape(tokens, width)

    near = spread_to(sources, "z").reshape(n_z, depth)
    half = spread_to(near, ("y", "x_lo", "x_hi")).reshape(tokens // n_c, depth)
    inputs = spread_to(half, "core").reshape(tokens, depth)

    preact = jnp.dot(inputs, enc_weight, preferred_element_type=jnp.float32) + enc_bias
    preact = preact.T
    feats = jax.nn.gelu(preact).astype(jnp.bfloat16)

    near_feats = spread_to(feats, "z").reshape(n_z * feats_own, tokens)
    all_feats = spread_to(near_feats, ("y", "x_lo")).reshape(rows, tokens)
    partial_value = lax.dot_general(
        all_feats, dec_weight, (((0,), (0,)), ((), ())), preferred_element_type=jnp.float32
    ).astype(jnp.bfloat16)
    parts = lax.all_gather(partial_value, FEAT, axis=0)
    outputs = jnp.sum(parts.astype(jnp.float32), axis=0) + dec_bias
    misfit = outputs - wanted.astype(jnp.float32)
    errors = (misfit * factor).astype(jnp.bfloat16)

    own_sq = jnp.broadcast_to(jnp.sum(misfit * misfit), (n_layer, 1, 128))
    every_sq = lax.all_to_all(own_sq, LAYER, split_axis=0, concat_axis=0, tiled=True)
    mse = jnp.sum(every_sq[:, 0, 0]) / (tokens * n_layer * width)

    grads = lax.dot_general(
        dec_weight, errors, (((1,), (1,)), ((), ())), preferred_element_type=jnp.float32
    ).astype(jnp.bfloat16)
    far = lax.all_to_all(
        grads.reshape(n_y * n_xl, n_z * feats_own, tokens), ("y", "x_lo"), split_axis=0, concat_axis=0, tiled=True
    )
    far = jnp.sum(far.astype(jnp.float32), axis=0).astype(jnp.bfloat16)
    close = lax.all_to_all(
        far.reshape(n_z, feats_own, tokens), "z", split_axis=0, concat_axis=0, tiled=True
    )
    feat_grad = jnp.sum(close.astype(jnp.float32), axis=0)

    dec_grad = jnp.dot(all_feats, errors, preferred_element_type=jnp.float32).astype(jnp.bfloat16)
    _, pullback = jax.vjp(jax.nn.gelu, preact)
    pre_grad = pullback(feat_grad)[0].astype(jnp.bfloat16)
    enc_grad = lax.dot_general(
        inputs, pre_grad, (((0,), (1,)), ((), ())), preferred_element_type=jnp.float32
    ).astype(jnp.bfloat16)
    return (enc_grad, dec_grad, mse)


def solution(mesh):
    n_layer, n_feat = mesh.devices.shape
    n_x_lo, n_z = 2, 8
    torus = Mesh(
        mesh.devices.reshape(n_layer // (n_x_lo * n_z), n_x_lo, n_z, n_feat // 2, 2), (*LAYER, *FEAT)
    )
    return jax.shard_map(
        per_device,
        mesh=torus,
        in_specs=(
            P((*LAYER, *FEAT), None),
            P((*LAYER, *FEAT), None),
            P(None, (*FEAT, *LAYER)),
            P((*FEAT, *LAYER)),
            P(FEAT, LAYER),
            P(LAYER),
        ),
        out_specs=(P(None, (*FEAT, *LAYER)), P(FEAT, LAYER), P()),
        check_vma=False,
    )
```

time: 1090 us -> 276 us (0.25)
  waiting for transfers between devices: 859 us -> 98.3 us
  blocking collectives: 168 us -> 98.1 us
  starting transfers between devices: 7.8 us -> 30.6 us
  matrix products: 36.3 us -> 19.7 us
  between operations: 15.6 us -> 2.64 us
  local copies, waits for them, and re-layouts: 4.17 us -> 16.4 us
    all_gather x2 -> x0, waiting for transfers between devices: 648 us -> none  [the longest x1 424 us: per_device(): inputs = lax.all_gather(sources, ('layer', 'feat'), axis=0, tiled=True)]
    reduce_scatter x1 -> x0, waiting for transfers between devices: 170 us -> none  [per_device(): lax.psum_scatter(lax.dot_general(dec_weight, errors, (((1,), (1,)), ((),...]
    psum x1 -> x0, blocking collectives: 160 us -> none  [per_device(): total_sq = lax.psum(jnp.sum(misfit * misfit), 'layer')]
    all_to_all x1 -> x6, waiting for transfers between devices: 0.01 us -> 98.3 us  [the longest x1 49.4 us: per_device(): lax.all_to_all(grads.reshape(n_y * n_xl, n_z * feats_own, tokens), ('y',...]
    all_gather x1 -> x2, blocking collectives: 7.28 us -> 53.2 us  [the longest x1 45.2 us: per_device(): lax.all_gather(owned.reshape(n_layer, width), FEAT, axis=0, tiled=True)]
    all_to_all x0 -> x3, blocking collectives: none -> 44.8 us  [spread_to(): lax.all_to_all(jnp.broadcast_to(block[None], (n, *block.shape)), axes, sp...]
    psum x1 -> x0, waiting for transfers between devices: 40.1 us -> none  [per_device(): lax.psum(partial_value.astype(jnp.bfloat16), 'feat').astype(jnp.float32)]
    all_to_all x1 -> x6, starting transfers between devices: 7.64 us -> 30.6 us  [the longest x2 12 us: spread_to(): lax.all_to_all(jnp.broadcast_to(block[None], (n, *block.shape)), axes, sp...]
  transfers between devices with their start and end apart: 5 -> 6, of which waited for: 4 -> 6; matrix products, arithmetic and copies ran while one was open for 1% -> 6% of each run, Pallas kernels for 0% -> 0%
where the time goes in v1:
time: 276 us; the launch traced here: 274 us
  waiting for transfers between devices  98.3 us (36%)
  blocking collectives  98.1 us (36%)
  starting transfers between devices  30.6 us (11%)
  matrix products  19.7 us (7%)
  local copies, waits for them, and re-layouts  16.4 us (6%)
  other arithmetic  7.86 us (3%)
    all_to_all x1, waiting for transfers between devices, per_device(): lax.all_to_all(grads.reshape(n_y * n_xl, n_z * feats_own, tokens), ('y',...  49.4 us
    all_gather x1, blocking collectives, per_device(): lax.all_gather(owned.reshape(n_layer, width), FEAT, axis=0, tiled=True)  45.2 us
    all_to_all x3, blocking collectives, spread_to(): lax.all_to_all(jnp.broadcast_to(block[None], (n, *block.shape)), axes, sp...  44.8 us
    all_to_all x2, waiting for transfers between devices, spread_to(): lax.all_to_all(jnp.broadcast_to(block[None], (n, *block.shape)), axes, sp...  27.2 us
    all_to_all x2, starting transfers between devices, spread_to(): lax.all_to_all(jnp.broadcast_to(block[None], (n, *block.shape)), axes, sp...  12 us
    all_to_all x1, waiting for transfers between devices, per_device(): lax.all_to_all(far.reshape(n_z, feats_own, tokens), 'z', split_axis=0, co...  8.74 us
    all_gather x1, blocking collectives, per_device(): parts = lax.all_gather(partial_value, FEAT, axis=0)  8.01 us
    all_to_all x1, waiting for transfers between devices, per_device(): lax.all_to_all(targets.reshape(n_layer, 1, width), LAYER, split_axis=0, c...  6.6 us
  transfers between devices with their start and end apart: 6, of which 6 were waited for; matrix products, arithmetic and copies ran while one was open for 6% of the time, Pallas kernels for 0%

profile of v1, /device:TPU:4, one launch (start us, length us, event | category | flops | bytes accessed | tf_op | source)
XLA Modules:
  0.0 273.5 jit_solution(3152163767902077613)
XLA Ops:
  0.6 0.0 copy-start
  0.6 1.0 reduce.3
  1.6 0.0 copy-start.2
  1.7 0.1 broadcast_in_dim.41
  1.8 0.5 broadcast.54
  2.3 1.4 reduce.4
  3.7 0.1 reshape.69
  3.8 17.4 %all_to_all.45 = bf16[8,2,4096]{2,1,0:T(2,128)(2,1)S(1)} all-to-all(bf16[8,2,4096]{2,1,0:T(2,128)(2,1)S(1)} %reshape.69), channel_id=1, replica_groups=mesh['y'=4,'x_lo'=2,'z'=8,'x_hi'=2,'core'=2] {'z'}, dimensions={0} | all-to-all | bytes 262144 | tf_op jit(solution)/shard_map/all_to_all | solution.py:14
  21.2 0.1 reshape.70
  21.3 0.2 copy.73
  21.5 1.5 broadcast_in_dim.43
  23.0 7.4 %all-to-all-start.1 = ((bf16[16,8,8192]{2,1,0:T(8,128)(2,1)}), bf16[16,8,8192]{2,1,0:T(8,128)(2,1)}, u32[]{:S(2)}, u32[]{:S(2)}) async-start(bf16[16,8,8192]{2,1,0:T(8,128)(2,1)} %broadcast_in_dim.43), calls=%async_computation.1 | async-start | bytes 4194304 | tf_op jit(solution)/shard_map/all_to_all | solution.py:14
  30.4 0.0 copy-done.2
  30.4 0.8 reduce.5
  31.3 0.6 reshape.71
  31.9 24.8 %all-to-all-done.1 = bf16[16,8,8192]{2,1,0:T(8,128)(2,1)} async-done(((bf16[16,8,8192]{2,1,0:T(8,128)(2,1)}), bf16[16,8,8192]{2,1,0:T(8,128)(2,1)}, u32[]{:S(2)}, u32[]{:S(2)}) %all-to-all-start.1) | async-done | bytes 2097184 | tf_op jit(solution)/shard_map/all_to_all | solution.py:14
  56.7 2.1 broadcast_in_dim.45
  58.8 0.0 copy-start.4
  58.8 8.2 %all_to_all.46 = bf16[2,128,8192]{2,1,0:T(8,128)(2,1)} all-to-all(bf16[2,128,8192]{2,1,0:T(8,128)(2,1)S(1)} %broadcast_in_dim.45), channel_id=1, replica_groups=mesh['y'=4,'x_lo'=2,'z'=8,'x_hi'=2,'core'=2] {'core'}, dimensions={0} | all-to-all | bytes 8388608 | tf_op jit(solution)/shard_map/all_to_all | solution.py:14
  66.9 4.6 %all-to-all-start.5 = ((bf16[64,2,128]{2,1,0:T(2,128)(2,1)}), bf16[64,2,128]{2,1,0:T(2,128)(2,1)S(1)}, u32[]{:S(2)}, u32[]{:S(2)}) async-start(bf16[64,2,128]{2,1,0:T(2,128)(2,1)} %reshape.71), calls=%async_computation.5 | async-start | bytes 65536 | tf_op jit(solution)/shard_map/all_to_all | solution.py:29
  71.6 0.0 copy-done
  71.6 0.0 copy-done.4
  71.6 3.7 %multiply_convert_fusion.1 = (bf16[128,256]{1,0:T(8,128)(2,1)S(1)}, f32[128,256]{1,0:T(8,128)S(1)}) fusion(f32[128]{0:T(128)S(1)} %copy-done.4, bf16[8192,128]{1,0:T(8,128)(2,1)S(1)} %copy-done, bf16[256,8192]{1,0:T(8,128)(2,1)} %bitcast.47), kind=kOutput, calls=%fused_computation.28 | convolution fusion | flops 537198592 | bytes 6488576 | tf_op jit(solution)/shard_map/dot_general | solution.py:37
  75.3 6.6 %all-to-all-done.5 = bf16[64,2,128]{2,1,0:T(2,128)(2,1)S(1)} async-done(((bf16[64,2,128]{2,1,0:T(2,128)(2,1)}), bf16[64,2,128]{2,1,0:T(2,128)(2,1)S(1)}, u32[]{:S(2)}, u32[]{:S(2)}) %all-to-all-start.5) | async-done | bytes 32800 | tf_op jit(solution)/shard_map/all_to_all | solution.py:29
  81.9 19.3 %all_to_all.47 = bf16[8,128,256]{2,1,0:T(8,128)(2,1)S(1)} all-to-all(bf16[8,128,256]{2,1,0:T(8,128)(2,1)S(1)} %broadcast_in_dim.46), channel_id=1, replica_groups=mesh['y'=4,'x_lo'=2,'z'=8,'x_hi'=2,'core'=2] {'z'}, dimensions={0} | all-to-all | bytes 1048576 | tf_op jit(solution)/shard_map/all_to_all | solution.py:14
  101.3 2.3 broadcast_in_dim.48
  103.5 4.5 %all-to-all-start.4 = ((bf16[8,1024,256]{2,1,0:T(8,128)(2,1)}), bf16[8,1024,256]{2,1,0:T(8,128)(2,1)}, u32[]{:S(2)}, u32[]{:S(2)}) async-start(bf16[8,1024,256]{2,1,0:T(8,128)(2,1)} %broadcast_in_dim.48), calls=%async_computation.4 | async-start | bytes 8388608 | tf_op jit(solution)/shard_map/all_to_all | solution.py:14
  108.1 45.2 %all-gather.1 = bf16[256,1,256]{2,0,1:T(8,128)(2,1)S(1)} all-gather(bf16[64,1,256]{2,0,1:T(8,128)(2,1)S(1)} %copy.44), channel_id=3, replica_groups=mesh['y'=4,'x_lo'=2,'z'=8,'x_hi'=2,'core'=2] {'x_hi','core'}, dimensions={0}, use_global_device_ids=true | all-gather | bytes 163840 | tf_op jit(solution)/shard_map/all_gather | solution.py:30
  153.4 2.4 all-to-all-done.4
  155.8 0.0 copy-start.3
  155.8 0.0 copy-start.1
  155.8 4.9 %convolution_convert_fusion.3 = bf16[256,256]{1,0:T(8,128)(2,1)S(1)} fusion(bf16[8192,256]{1,0:T(8,128)(2,1)} %bitcast.3, bf16[8192,256]{1,0:T(8,128)(2,1)} %param.10), kind=kOutput, calls=%fused_computation.5 | convolution fusion | flops 1073807360 | bytes 8519680 | tf_op jit(solution)/shard_map/dot_general | solution.py:43
  160.7 8.0 %all-gather = bf16[1024,256]{1,0:T(8,128)(2,1)S(1)} all-gather(bf16[256,256]{1,0:T(8,128)(2,1)S(1)} %convolution_convert_fusion.3), channel_id=2, replica_groups=mesh['y'=4,'x_lo'=2,'z'=8,'x_hi'=2,'core'=2] {'x_hi','core'}, dimensions={0}, use_global_device_ids=true | all-gather | bytes 655360 | tf_op jit(solution)/shard_map/all_gather | solution.py:46
  168.7 0.1 convert_reduce_fusion
  168.8 0.0 copy-done.3
  168.8 0.0 copy-done.1
  168.8 1.3 convolution_convert_fusion.1
  170.1 2.5 copy.72
  172.6 4.8 %all-to-all-start.6 = ((bf16[8,1024,256]{1,2,0:T(8,128)(2,1)}), bf16[8,1024,256]{1,2,0:T(8,128)(2,1)}, u32[]{:S(2)}, u32[]{:S(2)}) async-start(bf16[8,1024,256]{1,2,0:T(8,128)(2,1)} %bitcast.49), calls=%async_computation.6 | async-start | bytes 8388608 | tf_op jit(solution)/shard_map/all_to_all | solution.py:58
  177.4 0.7 multiply_reduce_fusion
  178.1 49.4 %all-to-all-done.6 = bf16[8,1024,256]{1,2,0:T(8,128)(2,1)} async-done(((bf16[8,1024,256]{1,2,0:T(8,128)(2,1)}), bf16[8,1024,256]{1,2,0:T(8,128)(2,1)}, u32[]{:S(2)}, u32[]{:S(2)}) %all-to-all-start.6) | async-done | bytes 4194336 | tf_op jit(solution)/shard_map/all_to_all | solution.py:58
  227.5 1.3 broadcast_in_dim.49
  228.8 5.5 %all-to-all-start.8 = ((f32[64,1,128]{2,1,0:T(1,128)}), f32[64,1,128]{2,1,0:T(1,128)S(1)}, u32[]{:S(2)}, u32[]{:S(2)}) async-start(f32[64,1,128]{2,1,0:T(1,128)} %broadcast_in_dim.49), calls=%async_computation.8 | async-start | bytes 65536 | tf_op jit(solution)/shard_map/all_to_all | solution.py:52
  234.3 3.1 %reduce_sum.51 = bf16[1024,256]{0,1:T(8,128)(2,1)S(1)} reduce(bf16[8,1024,256]{1,2,0:T(8,128)(2,1)} %all-to-all-done.6, bf16[]{:T(256)} %constant.17.clone.1), dimensions={0}, to_apply=%region_1.0 | reduce | flops 1835008 | bytes 4718594 | tf_op jit(solution)/shard_map/reduce_sum | solution.py:61
  237.4 0.9 copy_bitcast_fusion.1
  238.3 6.4 %all-to-all-done.8 = f32[64,1,128]{2,1,0:T(1,128)S(1)} async-done(((f32[64,1,128]{2,1,0:T(1,128)}), f32[64,1,128]{2,1,0:T(1,128)S(1)}, u32[]{:S(2)}, u32[]{:S(2)}) %all-to-all-start.8) | async-done | bytes 32800 | tf_op jit(solution)/shard_map/all_to_all | solution.py:52
  244.6 3.7 %all-to-all-start.7 = ((bf16[8,128,256]{1,2,0:T(8,128)(2,1)}), bf16[8,128,256]{1,2,0:T(8,128)(2,1)S(1)}, u32[]{:S(2)}, u32[]{:S(2)}) async-start(bf16[8,128,256]{1,2,0:T(8,128)(2,1)} %copy_bitcast_fusion.1), calls=%async_computation.7 | async-start | bytes 1048576 | tf_op jit(solution)/shard_map/all_to_all | solution.py:62
  248.3 5.5 %convolution_convert_fusion = bf16[8192,256]{1,0:T(8,128)(2,1)} fusion(bf16[8192,256]{1,0:T(8,128)(2,1)} %bitcast.3, bf16[256,256]{1,0:T(8,128)(2,1)S(1)} %bitcast.56), kind=kOutput, calls=%fused_computation | convolution fusion | flops 1075838976 | bytes 8519680 | tf_op jit(solution)/shard_map/dot_general | solution.py:67
  253.8 0.7 slice_reduce_fusion
  255.1 8.7 %all-to-all-done.7 = bf16[8,128,256]{1,2,0:T(8,128)(2,1)S(1)} async-done(((bf16[8,128,256]{1,2,0:T(8,128)(2,1)}), bf16[8,128,256]{1,2,0:T(8,128)(2,1)S(1)}, u32[]{:S(2)}, u32[]{:S(2)}) %all-to-all-start.7) | async-done | bytes 524320 | tf_op jit(solution)/shard_map/all_to_all | solution.py:62
  263.9 0.1 convert_reduce_fusion.1
  263.9 0.1 copy.50
  264.0 4.3 %fusion = bf16[8192,128]{0,1:T(8,128)(2,1)} fusion(bf16[256,8192]{1,0:T(8,128)(2,1)} %bitcast.48, f32[128,256]{1,0:T(8,128)S(1)} %get-tuple-element.27, f32[128,256]{1,0:T(8,128)S(1)} %copy.50), kind=kOutput, calls=%fused_computation.3 | convolution fusion | flops 538574848 | bytes 6553600 | tf_op jit(solution)/shard_map/dot_general | solution.py:70
  268.3 4.1 %copy.55 = bf16[8192,128]{1,0:T(8,128)(2,1)} copy(bf16[8192,128]{0,1:T(8,128)(2,1)} %fusion) | data formatting | bytes 4194304
  (7 shorter events, 0.1 us)
Async XLA Ops:
  0.6 70.9 %copy-start = (bf16[8192,128]{1,0:T(8,128)(2,1)S(1)}, bf16[8192,128]{1,0:T(8,128)(2,1)}, u32[]{:S(2)}) copy-start(bf16[8192,128]{1,0:T(8,128)(2,1)} %param.8) | copy-start | bytes 6291460
  1.6 28.8 %copy-start.2 = (bf16[1,16384]{1,0:T(2,128)(2,1)S(1)}, bf16[1,16384]{1,0:T(2,128)(2,1)}, u32[]{:S(2)}) copy-start(bf16[1,16384]{1,0:T(2,128)(2,1)} %param.7) | copy-start | bytes 98308
  23.0 33.7 %all-to-all-start.1 = ((bf16[16,8,8192]{2,1,0:T(8,128)(2,1)}), bf16[16,8,8192]{2,1,0:T(8,128)(2,1)}, u32[]{:S(2)}, u32[]{:S(2)}) async-start(bf16[16,8,8192]{2,1,0:T(8,128)(2,1)} %broadcast_in_dim.43), calls=%async_computation.1 | async-start | bytes 4194304 | tf_op jit(solution)/shard_map/all_to_all | solution.py:14
  58.8 12.8 %copy-start.4 = (f32[128]{0:T(128)S(1)}, f32[128]{0:T(128)}, u32[]{:S(2)}) copy-start(f32[128]{0:T(128)} %param.9) | copy-start | bytes 1540
  66.9 15.0 %all-to-all-start.5 = ((bf16[64,2,128]{2,1,0:T(2,128)(2,1)}), bf16[64,2,128]{2,1,0:T(2,128)(2,1)S(1)}, u32[]{:S(2)}, u32[]{:S(2)}) async-start(bf16[64,2,128]{2,1,0:T(2,128)(2,1)} %reshape.71), calls=%async_computation.5 | async-start | bytes 65536 | tf_op jit(solution)/shard_map/all_to_all | solution.py:29
  103.5 52.2 %all-to-all-start.4 = ((bf16[8,1024,256]{2,1,0:T(8,128)(2,1)}), bf16[8,1024,256]{2,1,0:T(8,128)(2,1)}, u32[]{:S(2)}, u32[]{:S(2)}) async-start(bf16[8,1024,256]{2,1,0:T(8,128)(2,1)} %broadcast_in_dim.48), calls=%async_computation.4 | async-start | bytes 8388608 | tf_op jit(solution)/shard_map/all_to_all | solution.py:14
  155.8 13.0 %copy-start.3 = (f32[256]{0:T(256)S(1)}, f32[256]{0:T(256)}, u32[]{:S(2)}) copy-start(f32[256]{0:T(256)} %param.11) | copy-start | bytes 3076
  155.8 13.0 %copy-start.1 = (bf16[8192,256]{1,0:T(8,128)(2,1)S(1)}, bf16[8192,256]{1,0:T(8,128)(2,1)}, u32[]{:S(2)}) copy-start(bf16[8192,256]{1,0:T(8,128)(2,1)} %param.10) | copy-start | bytes 12582916
  172.6 54.9 %all-to-all-start.6 = ((bf16[8,1024,256]{1,2,0:T(8,128)(2,1)}), bf16[8,1024,256]{1,2,0:T(8,128)(2,1)}, u32[]{:S(2)}, u32[]{:S(2)}) async-start(bf16[8,1024,256]{1,2,0:T(8,128)(2,1)} %bitcast.49), calls=%async_computation.6 | async-start | bytes 8388608 | tf_op jit(solution)/shard_map/all_to_all | solution.py:58
  228.8 15.9 %all-to-all-start.8 = ((f32[64,1,128]{2,1,0:T(1,128)}), f32[64,1,128]{2,1,0:T(1,128)S(1)}, u32[]{:S(2)}, u32[]{:S(2)}) async-start(f32[64,1,128]{2,1,0:T(1,128)} %broadcast_in_dim.49), calls=%async_computation.8 | async-start | bytes 65536 | tf_op jit(solution)/shard_map/all_to_all | solution.py:52
  244.6 19.2 %all-to-all-start.7 = ((bf16[8,128,256]{1,2,0:T(8,128)(2,1)}), bf16[8,128,256]{1,2,0:T(8,128)(2,1)S(1)}, u32[]{:S(2)}, u32[]{:S(2)}) async-start(bf16[8,128,256]{1,2,0:T(8,128)(2,1)} %copy_bitcast_fusion.1), calls=%async_computation.7 | async-start | bytes 1048576 | tf_op jit(solution)/shard_map/all_to_all | solution.py:62
